TPU v7x, 256 devices: a whole 4x4x8 slice. The times are simulated.
256 devices in a mesh: ctx: 32 (over y_lo, z, core), head: 8 (over y_hi, x).
Axes of the slice: x: 4, y: 4 (y_hi: 2, y_lo: 2; y = y_hi * 2 + y_lo), z: 8, core: 2. Of those that a mesh axis runs over, the one named last changes fastest.
Arguments:
- queries: bfloat16 [12288, 8, 6, 128], P('ctx', 'head'), may hold values from -5 to 5
- keys: bfloat16 [12288, 8, 128], P('ctx', 'head'), may hold values from -5 to 5
- values: bfloat16 [12288, 8, 128], P('ctx', 'head'), may hold values from -6 to 6
- d_out: bfloat16 [12288, 8, 6, 128], P('ctx', 'head'), may hold values from -45 to 45
- doc_block: int32 [96], replicated, may hold values from 0 to 23, never falling along the last dimension, each value on 1 to 12 neighbouring positions
- forget_flag: int32 [12288], P('ctx'), may hold values 0 or 1
Outputs:
- grad_queries: bfloat16 [12288, 8, 6, 128], P('ctx', 'head')
- grad_keys: bfloat16 [12288, 8, 128], P('ctx', 'head')
- grad_values: bfloat16 [12288, 8, 128], P('ctx', 'head')
Inputs may be any that keep to these rules, and one draw needn't show every extreme that they name: `doc_block`: document ids never fall along the blocks; each document spans 1 to 12 blocks, and one spans exactly 12.
All inputs are finite; a program needn't handle non-finite values. No bound on the sum of `forget_flag` on one device may be relied on, other than what follows from the above.
Results may differ from a plain program's by a relative error of at most 0.0075.
Values may be sent and summed in bfloat16 or wider, within the bound.
No kernel may reach another device: no remote copies, remote signals or barrier semaphores. Data moves between devices by JAX's collectives and lax.ppermute only.
A program may use at most 128 MiB of HBM per device.

v0:
```python
import math

import jax
import jax.numpy as jnp
from jax import lax
from jax.sharding import PartitionSpec as P

BLOCK = 128
REACH = 4


def shifted(x, axis, by):
    peers = lax.axis_size(axis)
    pairs = [(i, i + by) for i in range(peers) if 0 <= i + by < peers]
    return lax.ppermute(x, axis, pairs)


def for_sending(x):

    def short(part):
        return part.astype(jnp.bfloat16) if part.dtype == jnp.float32 else part

    return jax.tree.map(short, x)


def body(queries, keys, values, d_out, doc_block, forget_flag):
    tok_rows = queries.shape[0]
    key_heads = keys.shape[1]
    group_size = queries.shape[2]
    head_width = keys.shape[2]
    softmax_scale = 1.0 / math.sqrt(head_width)
    ctx_count = lax.axis_size("ctx")
    my_index = lax.axis_index("ctx")
    sign_rows = (1 - 2 * forget_flag).astype(jnp.bfloat16)
    out_grad = d_out * sign_rows[:, None, None, None]
    block_count = tok_rows // BLOCK
    token_iota = jnp.arange(tok_rows, dtype=jnp.int32)

    def token_docs(source_index):
        slice_start = jnp.maximum(source_index, 0) * block_count
        picked = lax.dynamic_slice_in_dim(doc_block, slice_start, block_count, 0)
        return jnp.repeat(picked, BLOCK, total_repeat_length=tok_rows)

    query_pos = my_index * tok_rows + token_iota
    query_doc = token_docs(my_index)

    def allowed_for(offset):
        source_index = my_index - offset
        key_pos = source_index * tok_rows + token_iota
        key_doc = token_docs(source_index)
        return (
            (key_pos[None, :] <= query_pos[:, None])
            & (key_doc[None, :] == query_doc[:, None])
            & (source_index >= 0)
        )

    def pair_scores(pair_kv, offset):
        allowed = allowed_for(offset)
        scores = (
            jnp.einsum("qhgd,khd->qhgk", queries, pair_kv[0], preferred_element_type=jnp.float32)
            * softmax_scale
        )
        scores = jnp.where(allowed[:, None, None, :], scores, -jnp.inf)
        slopes = jnp.einsum(
            "qhgd,khd->qhgk", out_grad, pair_kv[1], preferred_element_type=jnp.float32
        )
        return (scores, slopes)

    stacked = jnp.stack([keys, values])
    fetched = [stacked]
    for offset in range(1, REACH + 1):
        fetched.append(shifted(fetched[-1], "ctx", 1))
    scores, slopes = pair_scores(fetched[0], 0)
    running = jnp.max(scores, axis=-1)
    expo_terms = jnp.exp(scores - running[..., None])
    run_total = jnp.sum(expo_terms, axis=-1)
    weighted = jnp.sum(expo_terms * slopes, axis=-1)
    for offset in range(1, REACH + 1):

        def absorb(state_now, pair_kv=fetched[offset], offset=offset):
            run_max, run_sum, run_weighted = state_now
            pair_s, pair_slopes = pair_scores(pair_kv, offset)
            new_max = jnp.maximum(run_max, jnp.max(pair_s, axis=-1))
            factor = jnp.exp(run_max - new_max)
            pair_expo = jnp.exp(pair_s - new_max[..., None])
            return (
                new_max,
                run_sum * factor + jnp.sum(pair_expo, axis=-1),
                run_weighted * factor + jnp.sum(pair_expo * pair_slopes, axis=-1),
            )

        state_now = (running, run_total, weighted)
        state_now = absorb(state_now)
        running, run_total, weighted = state_now
    log_norm = running + jnp.log(run_total)
    row_delta = weighted / run_total

    def pair_grads(pair_kv, offset):
        pair_s, pair_slopes = pair_scores(pair_kv, offset)
        prob_full = jnp.exp(pair_s - log_norm[..., None])
        dscore = prob_full * (pair_slopes - row_delta[..., None])
        prob_half = prob_full.astype(jnp.bfloat16)
        dscore_half = dscore.astype(jnp.bfloat16)
        query_part = (
            jnp.einsum(
                "qhgk,khd->qhgd", dscore_half, pair_kv[0], preferred_element_type=jnp.float32
            )
            * softmax_scale
        )
        key_part = (
            jnp.einsum("qhgk,qhgd->khd", dscore_half, queries, preferred_element_type=jnp.float32)
            * softmax_scale
        )
        value_part = jnp.einsum(
            "qhgk,qhgd->khd", prob_half, out_grad, preferred_element_type=jnp.float32
        )
        return (query_part, jnp.stack([key_part, value_part]))

    query_sum, own_part = pair_grads(fetched[0], 0)
    remote_parts = []
    for offset in range(1, REACH + 1):

        def compute_pair(pair_kv, offset=offset):
            return pair_grads(pair_kv, offset)

        query_part, kv_part = compute_pair(fetched[offset])
        query_sum = query_sum + query_part
        remote_parts.append(kv_part)
    carried = jnp.zeros_like(own_part)
    for offset in range(REACH, 0, -1):
        carried = shifted(for_sending(carried + remote_parts[offset - 1]), "ctx", -1)
    kv_sum = own_part + carried
    local_squares = jnp.sum(query_sum * query_sum) + jnp.sum(kv_sum * kv_sum)
    square_total = lax.psum(local_squares, ("ctx", "head"))
    entries = (
        tok_rows * ctx_count * head_width * key_heads * lax.axis_size("head") * (group_size + 2)
    )
    norm_factor = lax.rsqrt(square_total / entries + 1e-06)
    return (
        (query_sum * norm_factor).astype(jnp.bfloat16),
        (kv_sum[0] * norm_factor).astype(jnp.bfloat16),
        (kv_sum[1] * norm_factor).astype(jnp.bfloat16),
    )


def solution(mesh):
    placed = (
        P("ctx", "head", None, None),
        P("ctx", "head", None),
        P("ctx", "head", None),
        P("ctx", "head", None, None),
        P(),
        P("ctx"),
    )
    return jax.shard_map(
        body,
        mesh=mesh,
        in_specs=placed,
        out_specs=(P("ctx", "head", None, None), P("ctx", "head", None), P("ctx", "head", None)),
        check_vma=False,
    )
```

profile of v0, /device:TPU:1, one launch (start us, length us, event | category | flops | bytes accessed | tf_op | source)
XLA Modules:
  0.0 200.9 jit_solution(6202212801447683181)
XLA Ops:
  1.7 4.9 %collective-permute-start = (bf16[2,384,1,128]{3,1,2,0:T(8,128)(2,1)S(1)}, bf16[2,384,1,128]{3,1,2,0:T(8,128)(2,1)S(1)}, u32[]{:S(2)}, u32[]{:S(2)}) collective-permute-start(bf16[2,384,1,128]{3,1,2,0:T(8,128)(2,1)S(1)} %pad_maximum_fusion), channel_id=1, source_target_pairs={{0,8},{8,16},{16,24},{24,32},{32,40},{40,48},{48,56},{56,64},{64,7... | collective-permute-start | bytes 589832 | tf_op jit(solution)/shard_map/ppermute | solution.py:15
  15.8 1.9 select_select_fusion
  17.8 1.9 select_select_fusion.4
  22.3 2.7 %fusion.15 = (f32[384,6]{0,1:T(8,128)S(1)}, f32[384,6]{0,1:T(8,128)S(1)}, f32[384,6,384]{0,2,1:T(8,128)}) fusion(f32[384,1,6,384]{0,3,2,1:T(8,128)S(1)} %get-tuple-element.153, f32[384,6]{0,1:T(8,128)S(1)} %get-tuple-element.152, bf16[384,1,128]{2,0,1:T(8,128)(2,1)S(1)} %copy-done.12, bf16[384,1,6,128]{3,0,2,1:T(8,128)(2,1)S(1)} %copy-done.1, ...), kind=kOutput, calls=%fused_computation.40 | convolution fusion | flops 230321664 | bytes 7794432 | tf_op jit(solution)/shard_map/qhgd,khd->qhgk/dot_general | solution.py:64
  25.0 1.9 collective-permute-start.1
  27.6 1.9 collective-permute-done.1
  29.5 4.4 %collective-permute-start.2 = (bf16[2,384,1,128]{3,1,2,0:T(8,128)(2,1)S(1)}, bf16[2,384,1,128]{3,1,2,0:T(8,128)(2,1)S(1)}, u32[]{:S(2)}, u32[]{:S(2)}) collective-permute-start(bf16[2,384,1,128]{3,1,2,0:T(8,128)(2,1)S(1)} %collective-permute-done.1), channel_id=1, source_target_pairs={{0,8},{8,16},{16,24},{24,32},{32,40},{40,48},{48,56},{56,64},{64,7... | collective-permute-start | bytes 589832 | tf_op jit(solution)/shard_map/ppermute | solution.py:15
  34.6 1.9 collective-permute-done.2
  36.5 4.6 %collective-permute-start.3 = (bf16[2,384,1,128]{3,1,2,0:T(8,128)(2,1)S(1)}, bf16[2,384,1,128]{3,1,2,0:T(8,128)(2,1)S(1)}, u32[]{:S(2)}, u32[]{:S(2)}) collective-permute-start(bf16[2,384,1,128]{3,1,2,0:T(8,128)(2,1)S(1)} %collective-permute-done.2), channel_id=1, source_target_pairs={{0,8},{8,16},{16,24},{24,32},{32,40},{40,48},{48,56},{56,64},{64,7... | collective-permute-start | bytes 589832 | tf_op jit(solution)/shard_map/ppermute | solution.py:15
  44.2 2.8 %fusion.19 = (f32[384,6]{0,1:T(8,128)S(1)}, f32[384,6]{0,1:T(8,128)S(1)}, f32[384,384,6]{1,0,2:T(8,128)}) fusion(f32[384,1,6,384]{0,3,2,1:T(8,128)S(1)} %get-tuple-element.147, f32[384,6]{0,1:T(8,128)S(1)} %get-tuple-element.108, bf16[384,1,6,128]{3,0,2,1:T(8,128)(2,1)S(1)} %copy-done.1, bf16[384]{0:T(512)(128)(2,1)S(1)} %subtract_convert_fusion, ...), kind=kOutput, calls=%fused_computation.44 | convolution fusion | flops 231206400 | bytes 7797760 | tf_op jit(solution)/shard_map/qhgd,khd->qhgk/dot_general | solution.py:64
  47.0 2.8 %fusion.18 = (f32[384,6]{0,1:T(8,128)S(1)}, f32[384,6]{0,1:T(8,128)S(1)}, f32[384,384,6]{1,0,2:T(8,128)}) fusion(f32[384,1,6,384]{0,3,2,1:T(8,128)S(1)} %get-tuple-element.149, f32[384,6]{0,1:T(8,128)S(1)} %get-tuple-element.109, bf16[384,1,6,128]{3,0,2,1:T(8,128)(2,1)S(1)} %copy-done.1, bf16[384]{0:T(512)(128)(2,1)S(1)} %subtract_convert_fusion, ...), kind=kOutput, calls=%fused_computation.43 | convolution fusion | flops 231206400 | bytes 7797760 | tf_op jit(solution)/shard_map/qhgd,khd->qhgk/dot_general | solution.py:64
  49.7 2.8 %fusion.17 = (f32[384,6]{0,1:T(8,128)S(1)}, f32[384,6]{0,1:T(8,128)S(1)}, f32[384,384,6]{1,0,2:T(8,128)}) fusion(f32[384,1,6,384]{0,3,2,1:T(8,128)S(1)} %get-tuple-element.151, f32[384,6]{0,1:T(8,128)S(1)} %get-tuple-element.110, bf16[384,1,6,128]{3,0,2,1:T(8,128)(2,1)S(1)} %copy-done.1, bf16[384]{0:T(512)(128)(2,1)S(1)} %subtract_convert_fusion, ...), kind=kOutput, calls=%fused_computation.42 | convolution fusion | flops 231206400 | bytes 7797760 | tf_op jit(solution)/shard_map/qhgd,khd->qhgk/dot_general | solution.py:64
  52.6 2.7 %fusion.16 = (f32[384,6]{0,1:T(8,128)S(1)}, f32[384,6]{0,1:T(8,128)S(1)}, f32[384,384,6]{1,0,2:T(8,128)}) fusion(f32[384,1,6,384]{0,3,2,1:T(8,128)S(1)} %get-tuple-element.155, f32[384,6]{0,1:T(8,128)S(1)} %get-tuple-element.111, bf16[384,1,6,128]{3,0,2,1:T(8,128)(2,1)S(1)} %copy-done.1, bf16[384]{0:T(512)(128)(2,1)S(1)} %subtract_convert_fusion, ...), kind=kOutput, calls=%fused_computation.41 | convolution fusion | flops 231206400 | bytes 7797760 | tf_op jit(solution)/shard_map/qhgd,khd->qhgk/dot_general | solution.py:64
  59.7 14.0 %fusion.44 = (bf16[384,6,384]{0,2,1:T(8,128)(2,1)}, bf16[384,6,384]{0,2,1:T(8,128)(2,1)}, bf16[384,6,384]{0,2,1:T(8,128)(2,1)}, bf16[384,6,384]{0,2,1:T(8,128)(2,1)}, bf16[384,6,384]{0,2,1:T(8,128)(2,1)}) fusion(f32[384,384,6]{1,0,2:T(8,128)} %get-tuple-element.156, f32[384,1,6,384]{0,3,2,1:T(8,128)} %copy-done.4, f32[384,6]{0,1:T(8,128)S(1)} %get-tuple-element.115, ...), kind=kLoop, calls=%fused_computation.64 | loop fusion | flops 17694720 | bytes 44255232 | tf_op jit(solution)/shard_map/reshape.186
  73.7 2.2 %fusion.86 = bf16[1,384,1,128]{3,1,2,0:T(8,128)(2,1)S(1)} fusion(bf16[384,6,384]{0,2,1:T(8,128)(2,1)} %get-tuple-element.116, bf16[384,1,6,128]{3,0,2,1:T(8,128)(2,1)S(1)} %copy-done), kind=kOutput, calls=%fused_computation.104 | convolution fusion | flops 226590720 | bytes 2457600 | tf_op jit(solution)/shard_map/qhgk,qhgd->khd/dot_general | solution.py:111
  75.9 2.3 %fusion.54 = f32[128,384,6]{0,1,2:T(8,128)S(1)} fusion(bf16[384,6,384]{0,2,1:T(8,128)(2,1)} %get-tuple-element.120, bf16[384,1,128]{2,0,1:T(8,128)(2,1)S(1)} %copy-done.10), kind=kOutput, calls=%fused_computation.79 | convolution fusion | flops 226787328 | bytes 3047424 | tf_op jit(solution)/shard_map/qhgk,khd->qhgd/dot_general | solution.py:105
  78.3 2.1 %collective-permute-start.4 = (bf16[2,384,1,128]{3,1,2,0:T(8,128)(2,1)S(1)}, bf16[2,384,1,128]{3,1,2,0:T(8,128)(2,1)S(1)}, u32[]{:S(2)}, u32[]{:S(2)}) collective-permute-start(bf16[2,384,1,128]{3,1,2,0:T(8,128)(2,1)S(1)} %pad_maximum_fusion.1), channel_id=1, source_target_pairs={{8,0},{16,8},{24,16},{32,24},{40,32},{48,40},{56,48},{64,56},{72,6... | collective-permute-start | bytes 589832 | tf_op jit(solution)/shard_map/ppermute | solution.py:15
  86.1 2.1 %collective-permute-start.5 = (bf16[2,384,1,128]{3,1,2,0:T(8,128)(2,1)S(1)}, bf16[2,384,1,128]{3,1,2,0:T(8,128)(2,1)S(1)}, u32[]{:S(2)}, u32[]{:S(2)}) collective-permute-start(bf16[2,384,1,128]{3,1,2,0:T(8,128)(2,1)S(1)} %fusion.113), channel_id=1, source_target_pairs={{8,0},{16,8},{24,16},{32,24},{40,32},{48,40},{56,48},{64,56},{72,6... | collective-permute-start | bytes 589832 | tf_op jit(solution)/shard_map/ppermute | solution.py:15
  88.8 4.4 %collective-permute-done.5 = bf16[2,384,1,128]{3,1,2,0:T(8,128)(2,1)S(1)} collective-permute-done((bf16[2,384,1,128]{3,1,2,0:T(8,128)(2,1)S(1)}, bf16[2,384,1,128]{3,1,2,0:T(8,128)(2,1)S(1)}, u32[]{:S(2)}, u32[]{:S(2)}) %collective-permute-start.5) | collective-permute-done | bytes 196640 | tf_op jit(solution)/shard_map/ppermute | solution.py:15
  93.2 1.9 collective-permute-start.6
  95.8 4.4 %collective-permute-done.6 = bf16[2,384,1,128]{3,1,2,0:T(8,128)(2,1)S(1)} collective-permute-done((bf16[2,384,1,128]{3,1,2,0:T(8,128)(2,1)S(1)}, bf16[2,384,1,128]{3,1,2,0:T(8,128)(2,1)S(1)}, u32[]{:S(2)}, u32[]{:S(2)}) %collective-permute-start.6) | collective-permute-done | bytes 196640 | tf_op jit(solution)/shard_map/ppermute | solution.py:15
  100.3 1.9 collective-permute-start.7
  102.8 4.4 %collective-permute-done.7 = bf16[2,384,1,128]{3,1,2,0:T(8,128)(2,1)S(1)} collective-permute-done((bf16[2,384,1,128]{3,1,2,0:T(8,128)(2,1)S(1)}, bf16[2,384,1,128]{3,1,2,0:T(8,128)(2,1)S(1)}, u32[]{:S(2)}, u32[]{:S(2)}) %collective-permute-start.7) | collective-permute-done | bytes 196640 | tf_op jit(solution)/shard_map/ppermute | solution.py:15
  109.3 89.3 %psum.7 = f32[]{:T(128)} all-reduce(f32[]{:T(128)S(6)} %add.306), channel_id=1, replica_groups=mesh['ctx'=32,'head'=8] {'ctx','head'}, use_global_device_ids=true, to_apply=%region_17.19 | all-reduce | flops 1 | bytes 8 | tf_op jit(solution)/shard_map/psum | solution.py:134
  (68 shorter events, 31.4 us)
Async XLA Ops:
  0.6 20.1 %copy-start = (bf16[384,1,6,128]{3,0,2,1:T(8,128)(2,1)S(1)}, bf16[384,1,6,128]{3,0,2,1:T(8,128)(2,1)}, u32[]{:S(2)}) copy-start(bf16[384,1,6,128]{3,0,2,1:T(8,128)(2,1)} %param.30) | copy-start | bytes 1769476
  0.6 21.7 %copy-start.12 = (bf16[384,1,128]{2,0,1:T(8,128)(2,1)S(1)}, bf16[384,1,128]{2,0,1:T(8,128)(2,1)}, u32[]{:S(2)}) copy-start(bf16[384,1,128]{2,0,1:T(8,128)(2,1)} %param.32) | copy-start | bytes 294916
  0.7 21.7 %copy-start.1 = (bf16[384,1,6,128]{3,0,2,1:T(8,128)(2,1)S(1)}, bf16[384,1,6,128]{3,0,2,1:T(8,128)(2,1)}, u32[]{:S(2)}) copy-start(bf16[384,1,6,128]{3,0,2,1:T(8,128)(2,1)} %param.33) | copy-start | bytes 1769476
  1.7 23.3 %collective-permute-start = (bf16[2,384,1,128]{3,1,2,0:T(8,128)(2,1)S(1)}, bf16[2,384,1,128]{3,1,2,0:T(8,128)(2,1)S(1)}, u32[]{:S(2)}, u32[]{:S(2)}) collective-permute-start(bf16[2,384,1,128]{3,1,2,0:T(8,128)(2,1)S(1)} %pad_maximum_fusion), channel_id=1, source_target_pairs={{0,8},{8,16},{16,24},{24,32},{32,40},{40,48},{48,56},{56,64},{64,7... | collective-permute-start | bytes 589832 | tf_op jit(solution)/shard_map/ppermute | solution.py:15
  25.0 4.5 %collective-permute-start.1 = (bf16[2,384,1,128]{3,1,2,0:T(8,128)(2,1)S(1)}, bf16[2,384,1,128]{3,1,2,0:T(8,128)(2,1)S(1)}, u32[]{:S(2)}, u32[]{:S(2)}) collective-permute-start(bf16[2,384,1,128]{3,1,2,0:T(8,128)(2,1)S(1)} %collective-permute-done), channel_id=1, source_target_pairs={{0,8},{8,16},{16,24},{24,32},{32,40},{40,48},{48,56},{56,64},{64,7... | collective-permute-start | bytes 589832 | tf_op jit(solution)/shard_map/ppermute | solution.py:15
  29.5 7.0 %collective-permute-start.2 = (bf16[2,384,1,128]{3,1,2,0:T(8,128)(2,1)S(1)}, bf16[2,384,1,128]{3,1,2,0:T(8,128)(2,1)S(1)}, u32[]{:S(2)}, u32[]{:S(2)}) collective-permute-start(bf16[2,384,1,128]{3,1,2,0:T(8,128)(2,1)S(1)} %collective-permute-done.1), channel_id=1, source_target_pairs={{0,8},{8,16},{16,24},{24,32},{32,40},{40,48},{48,56},{56,64},{64,7... | collective-permute-start | bytes 589832 | tf_op jit(solution)/shard_map/ppermute | solution.py:15
  34.6 23.5 %copy-start.2 = (f32[384,1,6,384]{0,3,2,1:T(8,128)}, f32[384,1,6,384]{0,3,2,1:T(8,128)S(1)}, u32[]{:S(2)}) copy-start(f32[384,1,6,384]{0,3,2,1:T(8,128)S(1)} %get-tuple-element.151) | copy-start | bytes 10616836
  36.5 7.0 %collective-permute-start.3 = (bf16[2,384,1,128]{3,1,2,0:T(8,128)(2,1)S(1)}, bf16[2,384,1,128]{3,1,2,0:T(8,128)(2,1)S(1)}, u32[]{:S(2)}, u32[]{:S(2)}) collective-permute-start(bf16[2,384,1,128]{3,1,2,0:T(8,128)(2,1)S(1)} %collective-permute-done.2), channel_id=1, source_target_pairs={{0,8},{8,16},{16,24},{24,32},{32,40},{40,48},{48,56},{56,64},{64,7... | collective-permute-start | bytes 589832 | tf_op jit(solution)/shard_map/ppermute | solution.py:15
  41.8 17.1 %copy-start.3 = (f32[384,1,6,384]{0,3,2,1:T(8,128)}, f32[384,1,6,384]{0,3,2,1:T(8,128)S(1)}, u32[]{:S(2)}) copy-start(f32[384,1,6,384]{0,3,2,1:T(8,128)S(1)} %get-tuple-element.149) | copy-start | bytes 10616836
  44.2 11.1 %copy-start.4 = (f32[384,1,6,384]{0,3,2,1:T(8,128)}, f32[384,1,6,384]{0,3,2,1:T(8,128)S(1)}, u32[]{:S(2)}) copy-start(f32[384,1,6,384]{0,3,2,1:T(8,128)S(1)} %get-tuple-element.147) | copy-start | bytes 10616836
  59.6 16.3 %copy-start.10 = (bf16[384,1,128]{2,0,1:T(8,128)(2,1)S(1)}, bf16[384,1,128]{2,0,1:T(8,128)(2,1)}, u32[]{:S(2)}) copy-start(bf16[384,1,128]{2,0,1:T(8,128)(2,1)} %param.31) | copy-start | bytes 294916
  73.7 4.6 %copy-start.11 = (bf16[1,384,1,128]{3,1,2,0:T(8,128)(2,1)S(1)}, bf16[1,384,1,128]{3,1,2,0:T(8,128)(2,1)}, u32[]{:S(2)}) copy-start(bf16[1,384,1,128]{3,1,2,0:T(8,128)(2,1)} %fusion.83) | copy-start | bytes 294916
  73.7 6.8 %copy-start.6 = (bf16[384,6,384]{0,2,1:T(8,128)(2,1)S(1)}, bf16[384,6,384]{0,2,1:T(8,128)(2,1)}, u32[]{:S(2)}) copy-start(bf16[384,6,384]{0,2,1:T(8,128)(2,1)} %get-tuple-element.117) | copy-start | bytes 5308420
  75.9 5.4 %copy-start.7 = (bf16[384,6,384]{0,2,1:T(8,128)(2,1)S(1)}, bf16[384,6,384]{0,2,1:T(8,128)(2,1)}, u32[]{:S(2)}) copy-start(bf16[384,6,384]{0,2,1:T(8,128)(2,1)} %get-tuple-element.118) | copy-start | bytes 5308420
  78.3 7.7 %collective-permute-start.4 = (bf16[2,384,1,128]{3,1,2,0:T(8,128)(2,1)S(1)}, bf16[2,384,1,128]{3,1,2,0:T(8,128)(2,1)S(1)}, u32[]{:S(2)}, u32[]{:S(2)}) collective-permute-start(bf16[2,384,1,128]{3,1,2,0:T(8,128)(2,1)S(1)} %pad_maximum_fusion.1), channel_id=1, source_target_pairs={{8,0},{16,8},{24,16},{32,24},{40,32},{48,40},{56,48},{64,56},{72,6... | collective-permute-start | bytes 589832 | tf_op jit(solution)/shard_map/ppermute | solution.py:15
  80.4 1.7 copy-start.8
  81.3 1.7 copy-start.9
  86.1 16.1 %copy-start.5 = (bf16[384,6,384]{0,2,1:T(8,128)(2,1)S(1)}, bf16[384,6,384]{0,2,1:T(8,128)(2,1)}, u32[]{:S(2)}) copy-start(bf16[384,6,384]{0,2,1:T(8,128)(2,1)} %get-tuple-element.120) | copy-start | bytes 5308420
  86.1 7.1 %collective-permute-start.5 = (bf16[2,384,1,128]{3,1,2,0:T(8,128)(2,1)S(1)}, bf16[2,384,1,128]{3,1,2,0:T(8,128)(2,1)S(1)}, u32[]{:S(2)}, u32[]{:S(2)}) collective-permute-start(bf16[2,384,1,128]{3,1,2,0:T(8,128)(2,1)S(1)} %fusion.113), channel_id=1, source_target_pairs={{8,0},{16,8},{24,16},{32,24},{40,32},{48,40},{56,48},{64,56},{72,6... | collective-permute-start | bytes 589832 | tf_op jit(solution)/shard_map/ppermute | solution.py:15
  93.2 7.0 %collective-permute-start.6 = (bf16[2,384,1,128]{3,1,2,0:T(8,128)(2,1)S(1)}, bf16[2,384,1,128]{3,1,2,0:T(8,128)(2,1)S(1)}, u32[]{:S(2)}, u32[]{:S(2)}) collective-permute-start(bf16[2,384,1,128]{3,1,2,0:T(8,128)(2,1)S(1)} %fusion.114), channel_id=1, source_target_pairs={{8,0},{16,8},{24,16},{32,24},{40,32},{48,40},{56,48},{64,56},{72,6... | collective-permute-start | bytes 589832 | tf_op jit(solution)/shard_map/ppermute | solution.py:15
  100.3 7.0 %collective-permute-start.7 = (bf16[2,384,1,128]{3,1,2,0:T(8,128)(2,1)S(1)}, bf16[2,384,1,128]{3,1,2,0:T(8,128)(2,1)S(1)}, u32[]{:S(2)}, u32[]{:S(2)}) collective-permute-start(bf16[2,384,1,128]{3,1,2,0:T(8,128)(2,1)S(1)} %fusion.115), channel_id=1, source_target_pairs={{8,0},{16,8},{24,16},{32,24},{40,32},{48,40},{56,48},{64,56},{72,6... | collective-permute-start | bytes 589832 | tf_op jit(solution)/shard_map/ppermute | solution.py:15
where the time goes:
time: 202 us; the launch traced here: 201 us
  blocking collectives  89.3 us (44%)
  matrix products  33.4 us (17%)
  other arithmetic  28.7 us (14%)
  starting transfers between devices  23.8 us (12%)
  waiting for transfers between devices  19.7 us (10%)
  between operations  3.13 us (2%)
  local copies, waits for them, and re-layouts  2.91 us (1%)
    psum x1, blocking collectives, body(): square_total = lax.psum(local_squares, ('ctx', 'head'))  89.3 us
    ppermute x8, starting transfers between devices, shifted(): return lax.ppermute(x, axis, pairs)  23.8 us
    ppermute x8, waiting for transfers between devices, shifted(): return lax.ppermute(x, axis, pairs)  19.7 us
    another operation x1, other arithmetic  14 us
    dot_general x5, matrix products, pair_scores(): jnp.einsum('qhgd,khd->qhgk', out_grad, pair_kv[1], preferred_element_type...  13.7 us
    select_n x5, other arithmetic, token_docs(): return jnp.repeat(picked, BLOCK, total_repeat_length=tok_rows)  9.46 us
    dot_general x5, matrix products, pair_grads(): jnp.einsum('qhgk,khd->qhgd', dscore_half, pair_kv[0], preferred_element_t...  6.26 us
    dot_general x5, matrix products, pair_grads(): jnp.einsum('qhgk,qhgd->khd', dscore_half, queries, preferred_element_type...  4.74 us
  transfers between devices with their start and end apart: 8, of which 7 were waited for; matrix products, arithmetic and copies ran while one was open for 13% of the time, Pallas kernels for 0%

commit v1 on v0

v1 whole, which is shorter than its diff:
```python
import functools
import math

import jax
import jax.numpy as jnp
from jax import lax
from jax.experimental import pallas as pl
from jax.experimental.pallas import tpu as pltpu
from jax.sharding import PartitionSpec as P

BLOCK = 128
REACH = 4
LOW = -1e30
F32 = jnp.float32
BF16 = jnp.bfloat16
NT = (((1,), (1,)), ((), ()))


def attn_kernel(
    blocks,
    chunks,
    me_ref,
    doc_ref,
    q_ref,
    do_ref,
    sign_ref,
    own_kv,
    kv_two,
    kv_four,
    sib_own,
    sib_two,
    sib_four,
    dq_ref,
    own_ref,
    two_ref,
    four_ref,
    cross_ref,
    sq_ref,
    win_k,
    win_v,
    s_ref,
    d_ref,
    m_ref,
    l_ref,
    w_ref,
    p_half,
    ds_half,
    q_rows,
    do_rows,
    q_turned,
    do_turned,
    dq_acc,
    dk_acc,
    dv_acc,
    sems,
):
    groups, tok_rows, width = q_ref.shape
    rows = groups * BLOCK
    shard = tok_rows
    scale = 1.0 / math.sqrt(width)
    expo = scale * math.log2(math.e)
    me = me_ref[0]
    core = lax.rem(me, 2)

    def fetch(source, slot_start, sem_index):
        start = pl.multiple_of(slot_start * shard, BLOCK)
        return (
            pltpu.make_async_copy(
                source.at[0], win_k.at[pl.ds(start, shard)], sems.at[sem_index, 0]
            ),
            pltpu.make_async_copy(
                source.at[1], win_v.at[pl.ds(start, shard)], sems.at[sem_index, 1]
            ),
        )

    copies = []
    copies += fetch(own_kv, REACH, 0)
    copies += fetch(kv_two, REACH - 2, 1)
    copies += fetch(kv_four, REACH - 4, 2)
    copies += fetch(sib_two, jnp.where(core == 0, REACH - 1, REACH - 3), 3)
    for copy in copies:
        copy.start()

    @pl.when(core == 0)
    def _():
        pair = fetch(sib_four, REACH - 3, 4)
        for copy in pair:
            copy.start()
        for copy in pair:
            copy.wait()

    @pl.when(core == 1)
    def _():
        pair = fetch(sib_own, REACH - 1, 4)
        for copy in pair:
            copy.start()
        for copy in pair:
            copy.wait()

    dk_acc[...] = jnp.zeros_like(dk_acc)
    dv_acc[...] = jnp.zeros_like(dv_acc)
    sq_ref[...] = jnp.zeros_like(sq_ref)
    for copy in copies:
        copy.wait()

    def one_block(b, carry):
        tok = pl.multiple_of(b * BLOCK, BLOCK)
        global_block = me * blocks + b
        my_doc = doc_ref[global_block]
        span = jnp.int32(1)
        for back in range(1, 2 * chunks):
            source = jnp.maximum(global_block - back, 0)
            same = (global_block >= back) & (doc_ref[source] == my_doc)
            span = span + same.astype(jnp.int32)
        steps = (span + 1) // 2
        last_block = REACH * blocks + b
        first_block = last_block + 1 - span
        for g in range(groups):
            at = slice(g * BLOCK, (g + 1) * BLOCK)
            q_part = q_ref[g, pl.ds(tok, BLOCK), :]
            do_part = do_ref[g, pl.ds(tok, BLOCK), :]
            q_rows[at, :] = q_part
            do_rows[at, :] = do_part
            q_turned[:, at] = q_part.T
            do_turned[:, at] = do_part.T

        def chunk_rows(step):
            return pl.multiple_of((last_block - 1 - 2 * step) * BLOCK, BLOCK)

        def raw_scores(step):
            k_pair = win_k[pl.ds(chunk_rows(step), 2 * BLOCK), :]
            return lax.dot_general(q_rows[...], k_pair, NT, preferred_element_type=F32)

        first = raw_scores(0)
        key_at = lax.broadcasted_iota(jnp.int32, (BLOCK, BLOCK), 1)
        tok_at = lax.broadcasted_iota(jnp.int32, (BLOCK, BLOCK), 0)
        causal = key_at <= tok_at
        before = last_block - 1 >= first_block
        for g in range(groups):
            at = slice(g * BLOCK, (g + 1) * BLOCK)
            far = jnp.where(before, first[at, :BLOCK], LOW)
            near = jnp.where(causal, first[at, BLOCK:], LOW)
            s_ref[0, at, :BLOCK] = far
            s_ref[0, at, BLOCK:] = near
            m_ref[at, :] = jnp.maximum(far, near)

        def score_step(step, c):
            scores = raw_scores(step)
            whole = last_block - 1 - 2 * step >= first_block
            for g in range(groups):
                at = slice(g * BLOCK, (g + 1) * BLOCK)
                far = jnp.where(whole, scores[at, :BLOCK], LOW)
                near = scores[at, BLOCK:]
                s_ref[step, at, :BLOCK] = far
                s_ref[step, at, BLOCK:] = near
                m_ref[at, :] = jnp.maximum(m_ref[at, :], jnp.maximum(far, near))
            return c

        lax.fori_loop(1, steps, score_step, 0)
        for g in range(groups):
            at = slice(g * BLOCK, (g + 1) * BLOCK)
            top = jnp.max(m_ref[at, :], axis=1, keepdims=True)
            m_ref[at, :] = jnp.broadcast_to(top, (BLOCK, BLOCK))
        l_ref[...] = jnp.zeros_like(l_ref)
        w_ref[...] = jnp.zeros_like(w_ref)

        def expo_step(step, c):
            v_pair = win_v[pl.ds(chunk_rows(step), 2 * BLOCK), :]
            slopes = lax.dot_general(do_rows[...], v_pair, NT, preferred_element_type=F32)
            for g in range(groups):
                at = slice(g * BLOCK, (g + 1) * BLOCK)
                top = m_ref[at, :]
                far = jnp.exp2((s_ref[step, at, :BLOCK] - top) * expo)
                near = jnp.exp2((s_ref[step, at, BLOCK:] - top) * expo)
                s_ref[step, at, :BLOCK] = far
                s_ref[step, at, BLOCK:] = near
                far_slope = slopes[at, :BLOCK]
                near_slope = slopes[at, BLOCK:]
                d_ref[step, at, :BLOCK] = far_slope
                d_ref[step, at, BLOCK:] = near_slope
                l_ref[at, :] += far + near
                w_ref[at, :] += far * far_slope + near * near_slope
            return c

        lax.fori_loop(0, steps, expo_step, 0)
        for g in range(groups):
            at = slice(g * BLOCK, (g + 1) * BLOCK)
            total = jnp.sum(l_ref[at, :], axis=1, keepdims=True)
            weighted = jnp.sum(w_ref[at, :], axis=1, keepdims=True)
            inverse = 1.0 / total
            w_ref[at, :] = jnp.broadcast_to(weighted * inverse, (BLOCK, BLOCK))
            l_ref[at, :] = inverse * sign_ref[pl.ds(tok, BLOCK), :]
        dq_acc[...] = jnp.zeros_like(dq_acc)

        def grad_step(step, c):
            for g in range(groups):
                at = slice(g * BLOCK, (g + 1) * BLOCK)
                inverse = l_ref[at, :]
                delta = w_ref[at, :]
                for half in (slice(0, BLOCK), slice(BLOCK, 2 * BLOCK)):
                    prob = s_ref[step, at, half] * inverse
                    p_half[at, half] = prob.astype(BF16)
                    ds_half[at, half] = (prob * (d_ref[step, at, half] - delta)).astype(BF16)
            k_pair = win_k[pl.ds(chunk_rows(step), 2 * BLOCK), :]
            dq_acc[...] += jnp.dot(ds_half[...], k_pair, preferred_element_type=F32)
            k_turned = jnp.dot(q_turned[...], ds_half[...], preferred_element_type=F32)
            v_turned = jnp.dot(do_turned[...], p_half[...], preferred_element_type=F32)
            low_block = last_block - 1 - 2 * step
            dk_acc[low_block] += k_turned[:, :BLOCK]
            dk_acc[low_block + 1] += k_turned[:, BLOCK:]
            dv_acc[low_block] += v_turned[:, :BLOCK]
            dv_acc[low_block + 1] += v_turned[:, BLOCK:]
            return c

        lax.fori_loop(0, steps, grad_step, 0)
        squares = jnp.zeros((BLOCK, width), F32)
        for g in range(groups):
            at = slice(g * BLOCK, (g + 1) * BLOCK)
            part = dq_acc[at, :] * scale
            dq_ref[g, pl.ds(tok, BLOCK), :] = part
            squares = squares + part * part
        sq_ref[...] += jnp.sum(squares.reshape(BLOCK // 8, 8, width), axis=0)
        return carry

    lax.fori_loop(0, blocks, one_block, 0)

    def emit(ref, lead, start_block):
        for i in range(blocks):
            ref[(*lead, 0, i)] = (dk_acc[start_block + i] * scale).astype(ref.dtype)
            ref[(*lead, 1, i)] = dv_acc[start_block + i].astype(ref.dtype)

    emit(own_ref, (), REACH * blocks)
    emit(two_ref, (), (REACH - 2) * blocks)
    emit(four_ref, (), (REACH - 4) * blocks)
    emit(cross_ref, (0,), jnp.where(core == 0, REACH - 1, REACH - 3) * blocks)
    emit(cross_ref, (1,), jnp.where(core == 0, REACH - 3, REACH - 1) * blocks)


def combine_kernel(me_ref, two_ref, four_ref, cross_ref, two_out, four_out):
    core = lax.rem(me_ref[0], 2)
    two_out[...] = (two_ref[...].astype(F32) + cross_ref[0].astype(F32)).astype(BF16)
    for kind in range(2):
        for i in range(four_ref.shape[1]):
            more = jnp.where(core == 1, cross_ref[1, kind, i].astype(F32), 0.0)
            four_out[kind, i] = (four_ref[kind, i].astype(F32) + more).astype(BF16)


def total_kernel(me_ref, own_ref, two_ref, four_ref, cross_ref, sq_ref, kv_out, sent_ref):
    core = lax.rem(me_ref[0], 2)
    squares = jnp.zeros(own_ref.shape[2:], F32)
    for kind in range(2):
        for i in range(own_ref.shape[1]):
            more = jnp.where(core == 0, cross_ref[1, kind, i].astype(F32), 0.0)
            whole = own_ref[kind, i] + more
            whole = whole + two_ref[kind, i].astype(F32) + four_ref[kind, i].astype(F32)
            squares = squares + whole * whole
            kv_out[kind, i * BLOCK : (i + 1) * BLOCK, :] = whole.T
    local = jnp.sum(squares) + jnp.sum(sq_ref[...])
    sent_ref[...] = jnp.full(sent_ref.shape, local, F32)


def finish_kernel(entries, got_ref, dq_ref, kv_ref, gq_ref, gk_ref, gv_ref):
    got = got_ref[...]
    total = jnp.sum(got) / got.shape[-1]
    norm = lax.rsqrt(jnp.full((1, 1), total / entries + 1e-06, F32))
    for g in range(dq_ref.shape[0]):
        gq_ref[g] = (dq_ref[g] * norm).astype(BF16)
    gk_ref[...] = (kv_ref[0] * norm).astype(BF16)
    gv_ref[...] = (kv_ref[1] * norm).astype(BF16)


def whole_specs(count):
    return [pl.BlockSpec(memory_space=pltpu.VMEM)] * count


def body(queries, keys, values, d_out, doc_block, forget_flag):
    tok_rows, _, groups, width = queries.shape
    blocks = tok_rows // BLOCK
    ctx_count = lax.axis_size("ctx")
    device_count = ctx_count * lax.axis_size("head")
    me = lax.axis_index("ctx").astype(jnp.int32).reshape(1)
    chunks = REACH * blocks // 2
    rows = groups * BLOCK

    def shifted(x, by):
        pairs = [(i, i + by) for i in range(ctx_count) if 0 <= i + by < ctx_count]
        return lax.ppermute(x, "ctx", pairs)

    def sibling(x):
        return lax.ppermute(x, "ctx", [(i, i ^ 1) for i in range(ctx_count)])

    q = queries.transpose(1, 2, 0, 3).reshape(groups, tok_rows, width)
    do = d_out.transpose(1, 2, 0, 3).reshape(groups, tok_rows, width)
    kv = jnp.stack([keys.reshape(tok_rows, width), values.reshape(tok_rows, width)])
    sign = (1 - 2 * forget_flag).astype(F32)
    sign = jnp.broadcast_to(sign[:, None], (tok_rows, BLOCK))
    kv_two = shifted(kv, 2)
    kv_four = shifted(kv, 4)
    sib_own = sibling(kv)
    sib_two = sibling(kv_two)
    sib_four = sibling(kv_four)

    smem = pl.BlockSpec(memory_space=pltpu.SMEM)
    anywhere = pl.BlockSpec(memory_space=pl.ANY)
    part = (2, blocks, width, BLOCK)
    window = (REACH + 1) * tok_rows
    dq, own, two, four, cross, sq = pl.pallas_call(
        functools.partial(attn_kernel, blocks, chunks),
        out_shape=(
            jax.ShapeDtypeStruct((groups, tok_rows, width), F32),
            jax.ShapeDtypeStruct(part, F32),
            jax.ShapeDtypeStruct(part, BF16),
            jax.ShapeDtypeStruct(part, BF16),
            jax.ShapeDtypeStruct((2, *part), BF16),
            jax.ShapeDtypeStruct((8, width), F32),
        ),
        in_specs=[smem, smem, *whole_specs(3), *[anywhere] * 6],
        out_specs=tuple(whole_specs(6)),
        scratch_shapes=[
            pltpu.VMEM((window, width), BF16),
            pltpu.VMEM((window, width), BF16),
            pltpu.VMEM((chunks, rows, 2 * BLOCK), F32),
            pltpu.VMEM((chunks, rows, 2 * BLOCK), F32),
            pltpu.VMEM((rows, BLOCK), F32),
            pltpu.VMEM((rows, BLOCK), F32),
            pltpu.VMEM((rows, BLOCK), F32),
            pltpu.VMEM((rows, 2 * BLOCK), BF16),
            pltpu.VMEM((rows, 2 * BLOCK), BF16),
            pltpu.VMEM((rows, width), BF16),
            pltpu.VMEM((rows, width), BF16),
            pltpu.VMEM((width, rows), BF16),
            pltpu.VMEM((width, rows), BF16),
            pltpu.VMEM((rows, width), F32),
            pltpu.VMEM(((REACH + 1) * blocks, width, BLOCK), F32),
            pltpu.VMEM(((REACH + 1) * blocks, width, BLOCK), F32),
            pltpu.SemaphoreType.DMA((5, 2)),
        ],
        name="attn",
    )(me, doc_block, q, do, sign, kv, kv_two, kv_four, sib_own, sib_two, sib_four)

    cross_in = sibling(cross)
    two_sum, four_sum = pl.pallas_call(
        combine_kernel,
        out_shape=(jax.ShapeDtypeStruct(part, BF16), jax.ShapeDtypeStruct(part, BF16)),
        in_specs=[smem, *whole_specs(3)],
        out_specs=tuple(whole_specs(2)),
        name="combine",
    )(me, two, four, cross_in)
    four_in = shifted(four_sum, -4)
    two_in = shifted(two_sum, -2)
    kv_sum, sent = pl.pallas_call(
        total_kernel,
        out_shape=(
            jax.ShapeDtypeStruct((2, tok_rows, width), F32),
            jax.ShapeDtypeStruct((device_count, 1, 128), F32),
        ),
        in_specs=[smem, *whole_specs(5)],
        out_specs=tuple(whole_specs(2)),
        name="total",
    )(me, own, two_in, four_in, cross_in, sq)
    got = lax.all_to_all(sent, ("ctx", "head"), 0, 0, tiled=True)
    entries = tok_rows * width * (groups + 2) * device_count
    gq, gk, gv = pl.pallas_call(
        functools.partial(finish_kernel, entries),
        out_shape=(
            jax.ShapeDtypeStruct((groups, tok_rows, width), BF16),
            jax.ShapeDtypeStruct((tok_rows, width), BF16),
            jax.ShapeDtypeStruct((tok_rows, width), BF16),
        ),
        in_specs=whole_specs(3),
        out_specs=tuple(whole_specs(3)),
        name="finish",
    )(got, dq, kv_sum)
    return (
        gq.reshape(1, groups, tok_rows, width).transpose(2, 0, 1, 3),
        gk.reshape(tok_rows, 1, width),
        gv.reshape(tok_rows, 1, width),
    )


def solution(mesh):
    placed = (
        P("ctx", "head", None, None),
        P("ctx", "head", None),
        P("ctx", "head", None),
        P("ctx", "head", None, None),
        P(),
        P("ctx"),
    )
    return jax.shard_map(
        body,
        mesh=mesh,
        in_specs=placed,
        out_specs=(P("ctx", "head", None, None), P("ctx", "head", None), P("ctx", "head", None)),
        check_vma=False,
    )
```

time: 202 us -> 99 us (0.49)
  blocking collectives: 89.3 us -> 40.2 us
  matrix products: 33.4 us -> 0 us
  other arithmetic: 28.7 us -> 1.65 us
  Pallas kernels: 0 us -> 17.1 us
  starting transfers between devices: 23.8 us -> 17.8 us
  between operations: 3.13 us -> 0.73 us
    psum x1 -> x0, blocking collectives: 89.3 us -> none  [body(): square_total = lax.psum(local_squares, ('ctx', 'head'))]
    all_to_all x0 -> x1, blocking collectives: none -> 40.2 us  [body(): got = lax.all_to_all(sent, ('ctx', 'head'), 0, 0, tiled=True)]
    dot_general x25 -> x0, matrix products: 33.4 us -> none  [the longest x5 13.7 us: pair_scores(): jnp.einsum('qhgd,khd->qhgk', out_grad, pair_kv[1], preferred_element_type...]
    pallas_call x0 -> x4, Pallas kernels: none -> 17.1 us  [the longest x1 10.1 us: body(): pl.pallas_call(functools.partial(attn_kernel, blocks, chunks), out_shape=...]
    another operation x3 -> x1, other arithmetic: 15.1 us -> 0.96 us  [body(): jnp.stack([keys.reshape(tok_rows, width), values.reshape(tok_rows, width)])]
    select_n x5 -> x0, other arithmetic: 9.46 us -> none  [token_docs(): return jnp.repeat(picked, BLOCK, total_repeat_length=tok_rows)]
    ppermute x8, starting transfers between devices: 23.8 us -> 17.8 us  [the longest x4 11.9 us: shifted(): return lax.ppermute(x, 'ctx', pairs)]
  transfers between devices with their start and end apart: 8 -> 8, of which waited for: 7 -> 5; matrix products, arithmetic and copies ran while one was open for 13% -> 1% of each run, Pallas kernels for 0% -> 0%
where the time goes in v1:
time: 99 us; the launch traced here: 99.1 us
  blocking collectives  40.2 us (41%)
  waiting for transfers between devices  19.4 us (20%)
  starting transfers between devices  17.8 us (18%)
  Pallas kernels  17.1 us (17%)
  local copies, waits for them, and re-layouts  2.23 us (2%)
  other arithmetic  1.65 us (2%)
    all_to_all x1, blocking collectives, body(): got = lax.all_to_all(sent, ('ctx', 'head'), 0, 0, tiled=True)  40.2 us
    ppermute x4, waiting for transfers between devices, shifted(): return lax.ppermute(x, 'ctx', pairs)  17.5 us
    ppermute x4, starting transfers between devices, shifted(): return lax.ppermute(x, 'ctx', pairs)  11.9 us
    pallas_call x1, Pallas kernels, body(): pl.pallas_call(functools.partial(attn_kernel, blocks, chunks), out_shape=...  10.1 us
    ppermute x4, starting transfers between devices, sibling(): return lax.ppermute(x, 'ctx', [(i, i ^ 1) for i in range(ctx_count)])  5.95 us
    pallas_call x1, Pallas kernels, body(): pl.pallas_call(functools.partial(finish_kernel, entries), out_shape=(jax....  2.7 us
    pallas_call x1, Pallas kernels, body(): pl.pallas_call(total_kernel, out_shape=(jax.ShapeDtypeStruct((2, tok_rows...  2.39 us
    pallas_call x1, Pallas kernels, body(): pl.pallas_call(combine_kernel, out_shape=(jax.ShapeDtypeStruct(part, BF16...  1.98 us
  transfers between devices with their start and end apart: 8, of which 5 were waited for; matrix products, arithmetic and copies ran while one was open for 1% of the time, Pallas kernels for 0%

profile of v1, /device:TPU:1, one launch (start us, length us, event | category | flops | bytes accessed | tf_op | source)
XLA Modules:
  0.0 99.1 jit_solution(9265518152153309734)
XLA Ops:
  0.6 1.0 pad_maximum_fusion.own_kv
  1.6 5.7 %collective-permute-start.1 = (bf16[2,384,128]{2,1,0:T(8,128)(2,1)S(1)}, bf16[2,384,128]{2,1,0:T(8,128)(2,1)S(1)}, u32[]{:S(2)}, u32[]{:S(2)}) collective-permute-start(bf16[2,384,128]{2,1,0:T(8,128)(2,1)S(1)} %pad_maximum_fusion.own_kv), channel_id=1, source_target_pairs={{0,32},{8,40},{16,48},{24,56},{32,64},{40,72},{48,80},{56,88},{64,... | collective-permute-start | bytes 589832 | tf_op jit(solution)/shard_map/ppermute | solution.py:287
  7.3 3.6 %collective-permute-start = (bf16[2,384,128]{2,1,0:T(8,128)(2,1)S(1)}, bf16[2,384,128]{2,1,0:T(8,128)(2,1)S(1)}, u32[]{:S(2)}, u32[]{:S(2)}) collective-permute-start(bf16[2,384,128]{2,1,0:T(8,128)(2,1)S(1)} %pad_maximum_fusion.own_kv), channel_id=1, source_target_pairs={{0,16},{8,24},{16,32},{24,40},{32,48},{40,56},{48,64},{56,72},{64,... | collective-permute-start | bytes 589832 | tf_op jit(solution)/shard_map/ppermute | solution.py:287
  10.9 1.3 %collective-permute-start.2 = (bf16[2,384,128]{2,1,0:T(8,128)(2,1)S(1)}, bf16[2,384,128]{2,1,0:T(8,128)(2,1)S(1)}, u32[]{:S(2)}, u32[]{:S(2)}) collective-permute-start(bf16[2,384,128]{2,1,0:T(8,128)(2,1)S(1)} %pad_maximum_fusion.own_kv), channel_id=1, source_target_pairs={{0,8},{8,0},{16,24},{24,16},{32,40},{40,32},{48,56},{56,48},{64,72... | collective-permute-start | bytes 589832 | tf_op jit(solution)/shard_map/ppermute | solution.py:290
  12.2 0.0 collective-permute-done.1.kv_four
  12.2 2.4 %collective-permute-start.4 = (bf16[2,384,128]{2,1,0:T(8,128)(2,1)S(1)}, bf16[2,384,128]{2,1,0:T(8,128)(2,1)S(1)}, u32[]{:S(2)}, u32[]{:S(2)}) collective-permute-start(bf16[2,384,128]{2,1,0:T(8,128)(2,1)S(1)} %collective-permute-done.1.kv_four), channel_id=1, source_target_pairs={{0,8},{8,0},{16,24},{24,16},{32,40},{40,32},{48,56},{56,48},{64,72... | collective-permute-start | bytes 589832 | tf_op jit(solution)/shard_map/ppermute | solution.py:290
  14.7 4.5 %collective-permute-done.kv_two = bf16[2,384,128]{2,1,0:T(8,128)(2,1)S(1)} collective-permute-done((bf16[2,384,128]{2,1,0:T(8,128)(2,1)S(1)}, bf16[2,384,128]{2,1,0:T(8,128)(2,1)S(1)}, u32[]{:S(2)}, u32[]{:S(2)}) %collective-permute-start) | collective-permute-done | bytes 196640 | tf_op jit(solution)/shard_map/ppermute | solution.py:287
  19.1 1.8 %collective-permute-start.3 = (bf16[2,384,128]{2,1,0:T(8,128)(2,1)S(1)}, bf16[2,384,128]{2,1,0:T(8,128)(2,1)S(1)}, u32[]{:S(2)}, u32[]{:S(2)}) collective-permute-start(bf16[2,384,128]{2,1,0:T(8,128)(2,1)S(1)} %collective-permute-done.kv_two), channel_id=1, source_target_pairs={{0,8},{8,0},{16,24},{24,16},{32,40},{40,32},{48,56},{56,48},{64,72... | collective-permute-start | bytes 589832 | tf_op jit(solution)/shard_map/ppermute | solution.py:290
  20.9 0.7 subtract_convert_fusion
  21.6 0.4 collective-permute-done.3.sib_two
  22.0 0.8 broadcast_in_dim.2.sign_ref
  22.8 10.1 %attn.1 = (f32[6,384,128]{2,1,0:T(8,128)}, f32[2,3,128,128]{3,2,1,0:T(8,128)}, bf16[2,3,128,128]{3,2,1,0:T(8,128)(2,1)}, bf16[2,3,128,128]{3,2,1,0:T(8,128)(2,1)...) custom-call(s32[1]{0:T(128)} %bitcast.me_ref, s32[96]{0:T(128)} %doc_ref.1, bf16[6,384,128]{2,1,0:T(8,128)(2,1)} %bitcast.14, ...), custom_call_target="tpu_custom_call" | custom-call | tf_op jit(solution)/shard_map/attn/pallas_call | solution.py:307
  32.9 0.5 collective-permute-start.5
  33.3 1.6 %collective-permute-done.5.cross_ref = bf16[2,2,3,128,128]{4,3,2,1,0:T(8,128)(2,1)S(1)} collective-permute-done((bf16[2,2,3,128,128]{4,3,2,1,0:T(8,128)(2,1)}, bf16[2,2,3,128,128]{4,3,2,1,0:T(8,128)(2,1)S(1)}, u32[]{:S(2)}, u32[]{:S(2)}) %collective-permute-start.5) | collective-permute-done | bytes 393248 | tf_op jit(solution)/shard_map/ppermute | solution.py:290
  34.9 0.7 copy-done
  35.6 2.0 %combine.1 = (bf16[2,3,128,128]{3,2,1,0:T(8,128)(2,1)}, bf16[2,3,128,128]{3,2,1,0:T(8,128)(2,1)}) custom-call(s32[1]{0:T(128)} %bitcast.me_ref, bf16[2,3,128,128]{3,2,1,0:T(8,128)(2,1)} %get-tuple-element.17.two_ref, bf16[2,3,128,128]{3,2,1,0:T(8,128)(2,1)} %get-tuple-element.18.four_ref, bf16[2,2,3,128,128]{4,3,2,1,0:T(8,128)(2,1)} %copy-done), custom_call_target="tpu_custom_call" | custom-call | tf_op jit(solution)/shard_map/combine/pallas_call | solution.py:342
  37.6 1.3 %collective-permute-start.6 = (bf16[2,3,128,128]{3,2,1,0:T(8,128)(2,1)}, bf16[2,3,128,128]{3,2,1,0:T(8,128)(2,1)S(1)}, u32[]{:S(2)}, u32[]{:S(2)}) collective-permute-start(bf16[2,3,128,128]{3,2,1,0:T(8,128)(2,1)} %get-tuple-element.20), channel_id=1, source_target_pairs={{16,0},{24,8},{32,16},{40,24},{48,32},{56,40},{64,48},{72,56},{80,... | collective-permute-start | bytes 589832 | tf_op jit(solution)/shard_map/ppermute | solution.py:287
  38.9 1.3 %collective-permute-start.7 = (bf16[2,3,128,128]{3,2,1,0:T(8,128)(2,1)}, bf16[2,3,128,128]{3,2,1,0:T(8,128)(2,1)S(1)}, u32[]{:S(2)}, u32[]{:S(2)}) collective-permute-start(bf16[2,3,128,128]{3,2,1,0:T(8,128)(2,1)} %get-tuple-element.21), channel_id=1, source_target_pairs={{32,0},{40,8},{48,16},{56,24},{64,32},{72,40},{80,48},{88,56},{96,... | collective-permute-start | bytes 589832 | tf_op jit(solution)/shard_map/ppermute | solution.py:287
  40.2 5.6 %collective-permute-done.6.two_ref = bf16[2,3,128,128]{3,2,1,0:T(8,128)(2,1)S(1)} collective-permute-done((bf16[2,3,128,128]{3,2,1,0:T(8,128)(2,1)}, bf16[2,3,128,128]{3,2,1,0:T(8,128)(2,1)S(1)}, u32[]{:S(2)}, u32[]{:S(2)}) %collective-permute-start.6) | collective-permute-done | bytes 196640 | tf_op jit(solution)/shard_map/ppermute | solution.py:287
  45.8 7.3 %collective-permute-done.7.four_ref = bf16[2,3,128,128]{3,2,1,0:T(8,128)(2,1)S(1)} collective-permute-done((bf16[2,3,128,128]{3,2,1,0:T(8,128)(2,1)}, bf16[2,3,128,128]{3,2,1,0:T(8,128)(2,1)S(1)}, u32[]{:S(2)}, u32[]{:S(2)}) %collective-permute-start.7) | collective-permute-done | bytes 196640 | tf_op jit(solution)/shard_map/ppermute | solution.py:287
  53.2 0.7 copy-done.8
  53.8 2.4 %total.1 = (f32[2,384,128]{2,1,0:T(8,128)}, f32[256,1,128]{2,1,0:T(1,128)}) custom-call(s32[1]{0:T(128)} %bitcast.me_ref, f32[2,3,128,128]{3,2,1,0:T(8,128)} %get-tuple-element.16.own_ref, bf16[2,3,128,128]{3,2,1,0:T(8,128)(2,1)} %copy-done.7, bf16[2,3,128,128]{3,2,1,0:T(8,128)(2,1)} %copy-done.8, bf16[2,2,3,128,128]{4,3,2,1,0:T(8,128)(2,1)} %copy-done, ...), custom_call_target="tpu_custom_call" | custom-call | tf_op jit(solution)/shard_map/total/pallas_call | solution.py:351
  56.2 40.2 %all_to_all.5.got_ref = f32[256,1,128]{2,1,0:T(1,128)} all-to-all(f32[256,1,128]{2,1,0:T(1,128)} %get-tuple-element.23), channel_id=1, replica_groups=mesh['ctx'=32,'head'=8] {'ctx','head'}, dimensions={0} | all-to-all | bytes 262144 | tf_op jit(solution)/shard_map/all_to_all | solution.py:361
  96.4 2.7 %finish.1 = (bf16[6,384,128]{2,1,0:T(8,128)(2,1)}, bf16[384,128]{1,0:T(8,128)(2,1)}, bf16[384,128]{1,0:T(8,128)(2,1)}) custom-call(f32[256,1,128]{2,1,0:T(1,128)} %all_to_all.5.got_ref, f32[6,384,128]{2,1,0:T(8,128)} %get-tuple-element.24.dq_ref, f32[2,384,128]{2,1,0:T(8,128)} %get-tuple-element.25.kv_ref), custom_call_target="tpu_custom_call" | custom-call | tf_op jit(solution)/shard_map/finish/pallas_call | solution.py:363
  (18 shorter events, 0.0 us)
Async XLA Ops:
  1.6 21.2 %copy-start.1 = (bf16[2,384,128]{2,1,0:T(8,128)(2,1)}, bf16[2,384,128]{2,1,0:T(8,128)(2,1)S(1)}, u32[]{:S(2)}) copy-start(bf16[2,384,128]{2,1,0:T(8,128)(2,1)S(1)} %pad_maximum_fusion.own_kv) | copy-start | bytes 589828
  1.6 10.6 %collective-permute-start.1 = (bf16[2,384,128]{2,1,0:T(8,128)(2,1)S(1)}, bf16[2,384,128]{2,1,0:T(8,128)(2,1)S(1)}, u32[]{:S(2)}, u32[]{:S(2)}) collective-permute-start(bf16[2,384,128]{2,1,0:T(8,128)(2,1)S(1)} %pad_maximum_fusion.own_kv), channel_id=1, source_target_pairs={{0,32},{8,40},{16,48},{24,56},{32,64},{40,72},{48,80},{56,88},{64,... | collective-permute-start | bytes 589832 | tf_op jit(solution)/shard_map/ppermute | solution.py:287
  7.3 11.8 %collective-permute-start = (bf16[2,384,128]{2,1,0:T(8,128)(2,1)S(1)}, bf16[2,384,128]{2,1,0:T(8,128)(2,1)S(1)}, u32[]{:S(2)}, u32[]{:S(2)}) collective-permute-start(bf16[2,384,128]{2,1,0:T(8,128)(2,1)S(1)} %pad_maximum_fusion.own_kv), channel_id=1, source_target_pairs={{0,16},{8,24},{16,32},{24,40},{32,48},{40,56},{48,64},{56,72},{64,... | collective-permute-start | bytes 589832 | tf_op jit(solution)/shard_map/ppermute | solution.py:287
  10.9 10.7 %collective-permute-start.2 = (bf16[2,384,128]{2,1,0:T(8,128)(2,1)S(1)}, bf16[2,384,128]{2,1,0:T(8,128)(2,1)S(1)}, u32[]{:S(2)}, u32[]{:S(2)}) collective-permute-start(bf16[2,384,128]{2,1,0:T(8,128)(2,1)S(1)} %pad_maximum_fusion.own_kv), channel_id=1, source_target_pairs={{0,8},{8,0},{16,24},{24,16},{32,40},{40,32},{48,56},{56,48},{64,72... | collective-permute-start | bytes 589832 | tf_op jit(solution)/shard_map/ppermute | solution.py:290
  12.2 10.5 %copy-start.2 = (bf16[2,384,128]{2,1,0:T(8,128)(2,1)}, bf16[2,384,128]{2,1,0:T(8,128)(2,1)S(1)}, u32[]{:S(2)}) copy-start(bf16[2,384,128]{2,1,0:T(8,128)(2,1)S(1)} %collective-permute-done.1.kv_four) | copy-start | bytes 589828
  12.2 9.4 %collective-permute-start.4 = (bf16[2,384,128]{2,1,0:T(8,128)(2,1)S(1)}, bf16[2,384,128]{2,1,0:T(8,128)(2,1)S(1)}, u32[]{:S(2)}, u32[]{:S(2)}) collective-permute-start(bf16[2,384,128]{2,1,0:T(8,128)(2,1)S(1)} %collective-permute-done.1.kv_four), channel_id=1, source_target_pairs={{0,8},{8,0},{16,24},{24,16},{32,40},{40,32},{48,56},{56,48},{64,72... | collective-permute-start | bytes 589832 | tf_op jit(solution)/shard_map/ppermute | solution.py:290
  19.1 3.6 %copy-start.3 = (bf16[2,384,128]{2,1,0:T(8,128)(2,1)}, bf16[2,384,128]{2,1,0:T(8,128)(2,1)S(1)}, u32[]{:S(2)}) copy-start(bf16[2,384,128]{2,1,0:T(8,128)(2,1)S(1)} %collective-permute-done.kv_two) | copy-start | bytes 589828
  19.1 2.8 %collective-permute-start.3 = (bf16[2,384,128]{2,1,0:T(8,128)(2,1)S(1)}, bf16[2,384,128]{2,1,0:T(8,128)(2,1)S(1)}, u32[]{:S(2)}, u32[]{:S(2)}) collective-permute-start(bf16[2,384,128]{2,1,0:T(8,128)(2,1)S(1)} %collective-permute-done.kv_two), channel_id=1, source_target_pairs={{0,8},{8,0},{16,24},{24,16},{32,40},{40,32},{48,56},{56,48},{64,72... | collective-permute-start | bytes 589832 | tf_op jit(solution)/shard_map/ppermute | solution.py:290
  21.6 1.2 %copy-start.4 = (bf16[2,384,128]{2,1,0:T(8,128)(2,1)}, bf16[2,384,128]{2,1,0:T(8,128)(2,1)S(1)}, u32[]{:S(2)}) copy-start(bf16[2,384,128]{2,1,0:T(8,128)(2,1)S(1)} %collective-permute-done.2.sib_own) | copy-start | bytes 589828
  21.6 1.2 %copy-start.5 = (bf16[2,384,128]{2,1,0:T(8,128)(2,1)}, bf16[2,384,128]{2,1,0:T(8,128)(2,1)S(1)}, u32[]{:S(2)}) copy-start(bf16[2,384,128]{2,1,0:T(8,128)(2,1)S(1)} %collective-permute-done.4.sib_four) | copy-start | bytes 589828
  22.0 0.8 copy-start.6
  32.9 2.0 %collective-permute-start.5 = (bf16[2,2,3,128,128]{4,3,2,1,0:T(8,128)(2,1)}, bf16[2,2,3,128,128]{4,3,2,1,0:T(8,128)(2,1)S(1)}, u32[]{:S(2)}, u32[]{:S(2)}) collective-permute-start(bf16[2,2,3,128,128]{4,3,2,1,0:T(8,128)(2,1)} %get-tuple-element.19), channel_id=1, source_target_pairs={{0,8},{8,0},{16,24},{24,16},{32,40},{40,32},{48,56},{56,48},{64,72... | collective-permute-start | bytes 1179656 | tf_op jit(solution)/shard_map/ppermute | solution.py:290
  34.9 0.7 copy-start
  37.6 8.2 %collective-permute-start.6 = (bf16[2,3,128,128]{3,2,1,0:T(8,128)(2,1)}, bf16[2,3,128,128]{3,2,1,0:T(8,128)(2,1)S(1)}, u32[]{:S(2)}, u32[]{:S(2)}) collective-permute-start(bf16[2,3,128,128]{3,2,1,0:T(8,128)(2,1)} %get-tuple-element.20), channel_id=1, source_target_pairs={{16,0},{24,8},{32,16},{40,24},{48,32},{56,40},{64,48},{72,56},{80,... | collective-permute-start | bytes 589832 | tf_op jit(solution)/shard_map/ppermute | solution.py:287
  38.9 14.3 %collective-permute-start.7 = (bf16[2,3,128,128]{3,2,1,0:T(8,128)(2,1)}, bf16[2,3,128,128]{3,2,1,0:T(8,128)(2,1)S(1)}, u32[]{:S(2)}, u32[]{:S(2)}) collective-permute-start(bf16[2,3,128,128]{3,2,1,0:T(8,128)(2,1)} %get-tuple-element.21), channel_id=1, source_target_pairs={{32,0},{40,8},{48,16},{56,24},{64,32},{72,40},{80,48},{88,56},{96,... | collective-permute-start | bytes 589832 | tf_op jit(solution)/shard_map/ppermute | solution.py:287
  45.8 7.4 %copy-start.7 = (bf16[2,3,128,128]{3,2,1,0:T(8,128)(2,1)}, bf16[2,3,128,128]{3,2,1,0:T(8,128)(2,1)S(1)}, u32[]{:S(2)}) copy-start(bf16[2,3,128,128]{3,2,1,0:T(8,128)(2,1)S(1)} %collective-permute-done.6.two_ref) | copy-start | bytes 589828
  53.2 0.7 copy-start.8
